TPU v7x, 256 devices: a whole 4x4x8 slice. The times are simulated.
256 devices in a mesh: seq: 64 (over x, z, core), tp: 4 (over y).
Axes of the slice: x: 4, y: 4, z: 8, core: 2. Of those that a mesh axis runs over, the one named last changes fastest.
Arguments:
- hidden_states: bfloat16 [16384, 3584], P('seq', 'tp'), may hold values from -6 to 6
- queries: bfloat16 [16384, 3584], P('seq', 'tp'), may hold values from -6 to 6
- key_weight: bfloat16 [3584, 512], P(None, 'tp'), may hold values from -0.09375 to 0.09375
- value_weight: bfloat16 [3584, 512], P(None, 'tp'), may hold values from -0.09375 to 0.09375
- output_weight: bfloat16 [3584, 3584], P('tp'), may hold values from -1.5 to 1.5
- prefix_keys: bfloat16 [16384, 512], P('seq', 'tp'), may hold values from -64 to 64
- prefix_values: bfloat16 [16384, 512], P('seq', 'tp'), may hold values from -6 to 6
- reads: int32 [64, 16], replicated, may hold values from 0 to 255, as said below
- out_grad: bfloat16 [16384, 3584], P('seq', 'tp'), may hold values from -6 to 6
Outputs:
- layer_output: bfloat16 [16384, 3584], P('seq', 'tp')
- prefix_key_grad: float32 [16384, 512], P('seq', 'tp')
- prefix_value_grad: float32 [16384, 512], P('seq', 'tp')
Inputs may be any that keep to these rules, and one draw needn't show every extreme that they name: Entry l of a row is the row's node at depth l of a prefix tree, one of the blocks l * (16) to (l + 1) * 16 - 1; two rows that share a node share all its ancestors, and all rows share the root. Block b is held by index b // 4 of seq; every row names exactly 1 block of each index that it reads from.
All inputs are finite; a program needn't handle non-finite values.
Results may differ from a plain program's by a relative error of at most 0.0095.
Values may be sent and summed in bfloat16 or wider, within the bound.
A program may use at most 128 MiB of HBM per device.

v0:
```python
import jax
import jax.numpy as jnp
from jax import lax
from jax.sharding import PartitionSpec as P

QH = 28
KVH = 4
HD = 128
PBLK = 64


def local(
    hidden_states,
    queries,
    key_weight,
    value_weight,
    output_weight,
    prefix_keys,
    prefix_values,
    reads,
    out_grad,
):
    length = hidden_states.shape[0]
    scaling = HD ** (-0.5)
    groups = QH // KVH
    cache_cols = key_weight.shape[1]
    seq_count = lax.axis_size("seq")
    own_index = lax.axis_index("seq")
    blocks_here = prefix_keys.shape[0] // PBLK
    flat_width = PBLK * 2 * cache_cols
    read_count = reads.shape[1]
    hidden_piece = lax.all_gather(hidden_states, "tp", axis=1, tiled=True)
    grad_piece = lax.all_gather(out_grad, "tp", axis=1, tiled=True)
    new_keys = jnp.dot(hidden_piece, key_weight, preferred_element_type=jnp.float32)
    new_values = jnp.dot(hidden_piece, value_weight, preferred_element_type=jnp.float32)
    context_grad = lax.dot_general(
        grad_piece, output_weight, (((1,), (1,)), ((), ())), preferred_element_type=jnp.float32
    )
    new_keys = new_keys.astype(jnp.bfloat16)
    new_values = new_values.astype(jnp.bfloat16)
    context_grad = context_grad.astype(jnp.bfloat16)
    my_reads = lax.dynamic_slice_in_dim(reads, own_index, 1, 0)[0]
    local_cache = jnp.concatenate([prefix_keys, prefix_values], axis=1).reshape(
        blocks_here, flat_width
    )
    everything = lax.all_gather(local_cache, "seq", axis=0, tiled=True)
    fetched = jnp.take(everything, my_reads, axis=0)
    fetched_rows = fetched.reshape(read_count * PBLK, 2 * cache_cols)
    causal = jnp.arange(length)[None, :] <= jnp.arange(length)[:, None]
    context_parts = []
    keys_prefix = fetched_rows[:, 0:HD]
    values_prefix = fetched_rows[:, cache_cols : cache_cols + HD]
    key_total = jnp.zeros((read_count * PBLK, HD), jnp.float32)
    value_total = jnp.zeros((read_count * PBLK, HD), jnp.float32)
    for member in range(groups):
        column = member * HD
        head_queries = queries[:, column : column + HD]
        head_grads = context_grad[:, column : column + HD]
        scores_prefix = (
            jnp.einsum("td,pd->tp", head_queries, keys_prefix, preferred_element_type=jnp.float32)
            * scaling
        )
        scores_own = (
            jnp.einsum("td,ud->tu", head_queries, new_keys, preferred_element_type=jnp.float32)
            * scaling
        )
        masked_own = jnp.where(causal, scores_own, -jnp.inf)
        peak_score = jnp.maximum(jnp.max(scores_prefix, axis=-1), jnp.max(masked_own, axis=-1))[
            :, None
        ]
        exps_prefix = jnp.exp(scores_prefix - peak_score)
        exps_own = jnp.exp(masked_own - peak_score)
        denominator = (jnp.sum(exps_prefix, axis=-1) + jnp.sum(exps_own, axis=-1))[:, None]
        softmax_prefix = exps_prefix / denominator
        softmax_own = exps_own / denominator
        weights_prefix = softmax_prefix.astype(jnp.bfloat16)
        weights_own = softmax_own.astype(jnp.bfloat16)
        context = jnp.dot(weights_prefix, values_prefix, preferred_element_type=jnp.float32)
        context = context + jnp.dot(weights_own, new_values, preferred_element_type=jnp.float32)
        context_parts.append(context.astype(jnp.bfloat16))
        slope_prefix = jnp.einsum(
            "td,pd->tp", head_grads, values_prefix, preferred_element_type=jnp.float32
        )
        slope_own = jnp.einsum(
            "td,ud->tu", head_grads, new_values, preferred_element_type=jnp.float32
        )
        row_delta = jnp.sum(softmax_prefix * slope_prefix, axis=-1) + jnp.sum(
            softmax_own * slope_own, axis=-1
        )
        score_grad = (softmax_prefix * (slope_prefix - row_delta[:, None])).astype(jnp.bfloat16)
        value_total = value_total + jnp.einsum(
            "tp,td->pd", weights_prefix, head_grads, preferred_element_type=jnp.float32
        )
        key_total = key_total + jnp.einsum(
            "tp,td->pd", score_grad, head_queries, preferred_element_type=jnp.float32
        )
    key_parts = [key_total * scaling]
    value_parts = [value_total]
    attention = jnp.concatenate(context_parts, axis=1)
    cache_grads = jnp.concatenate(key_parts + value_parts, axis=1).reshape(read_count, flat_width)
    partial_value = jnp.dot(attention, output_weight, preferred_element_type=jnp.float32)
    layer_output = lax.psum_scatter(
        partial_value.astype(jnp.bfloat16), "tp", scatter_dimension=1, tiled=True
    )
    spread = (
        jnp.zeros((seq_count * blocks_here, flat_width), jnp.float32).at[my_reads].set(cache_grads)
    )
    summed = lax.psum_scatter(spread, "seq", scatter_dimension=0, tiled=True)
    summed_rows = summed.reshape(blocks_here * PBLK, 2 * cache_cols)
    return (layer_output, summed_rows[:, :cache_cols], summed_rows[:, cache_cols:])


def solution(mesh):
    in_specs = (
        P("seq", "tp"),
        P("seq", "tp"),
        P(None, "tp"),
        P(None, "tp"),
        P("tp", None),
        P("seq", "tp"),
        P("seq", "tp"),
        P(),
        P("seq", "tp"),
    )
    out_specs = (P("seq", "tp"), P("seq", "tp"), P("seq", "tp"))
    return jax.shard_map(local, mesh=mesh, in_specs=in_specs, out_specs=out_specs, check_vma=False)
```

profile of v0, /device:TPU:1, one launch (start us, length us, event | category | flops | bytes accessed | tf_op | source)
XLA Modules:
  0.0 477.5 jit_solution(8328261768748343851)
XLA Ops:
  11.5 33.5 %all-gather.5.cloned.1.call-done = bf16[256,3584]{1,0:T(8,128)(2,1)} async-done(((bf16[256,896]{1,0:T(8,128)(2,1)}), bf16[256,3584]{1,0:T(8,128)(2,1)}) %all-gather.5.cloned.1.call-update) | async-done | bytes 1835024 | tf_op jit(solution)/shard_map/all_gather | solution.py:32
  45.0 2.1 convolution_convert_fusion.3
  47.1 1.7 fusion.211
  48.8 1.7 fusion.213
  50.6 1.1 fusion.215
  51.6 1.1 fusion.217
  52.7 1.1 fusion.219
  54.2 2.1 convolution_convert_fusion.2
  56.3 21.7 %all-gather.7.cloned.1.call-done = bf16[256,3584]{1,0:T(8,128)(2,1)} async-done(((bf16[256,896]{1,0:T(8,128)(2,1)}), bf16[256,3584]{1,0:T(8,128)(2,1)}) %all-gather.7.cloned.1.call-update) | async-done | bytes 1835024 | tf_op jit(solution)/shard_map/all_gather | solution.py:33
  78.1 6.2 %convolution_convert_fusion.1 = bf16[256,896]{1,0:T(8,128)(2,1)} fusion(bf16[256,3584]{1,0:T(8,128)(2,1)} %all-gather.7.cloned.1.call-done, bf16[896,3584]{1,0:T(8,128)(2,1)} %param.13), kind=kOutput, calls=%fused_computation.12 | convolution fusion | flops 1644396544 | bytes 8716288 | tf_op jit(solution)/shard_map/dot_general | solution.py:36
  84.3 80.6 %all-gather.9.cloned.1.call-done = bf16[64,4,16384]{2,1,0:T(4,128)(2,1)} async-done(((bf16[1,4,16384]{2,1,0:T(4,128)(2,1)}), bf16[64,4,16384]{2,1,0:T(4,128)(2,1)}) %all-gather.9.cloned.1.call-update) | async-done | bytes 8388624 | tf_op jit(solution)/shard_map/all_gather | solution.py:46
  164.9 12.5 %reshape.177 = bf16[256,16384]{1,0:T(8,128)(2,1)} reshape(bf16[64,4,16384]{2,1,0:T(4,128)(2,1)} %all-gather.9.cloned.1.call-done) | data formatting | bytes 16777216
  177.4 5.8 %gather_fusion = bf16[16,16384]{1,0:T(8,128)(2,1)S(1)} fusion(bf16[256,16384]{1,0:T(8,128)(2,1)} %reshape.177, s32[1024]{0:T(1024)S(1)} %pad_clamp_fusion), kind=kCustom, calls=%fused_computation | custom fusion | bytes 1048640 | tf_op jit(solution)/shard_map/jit(_take)/gather | solution.py:47
  186.5 1.2 fusion.81
  187.7 1.4 fusion.50
  190.0 1.3 fusion.48
  192.1 1.3 fusion.46
  194.1 1.4 fusion.44
  196.2 1.3 fusion.42
  198.3 1.3 fusion.40
  200.3 1.3 fusion.38
  204.2 1.0 slice-done
  206.1 2.3 convolution_convert_fusion
  208.4 2.3 copy.63
  210.8 1.8 convolution_add_fusion.5
  213.0 1.7 convolution_add_fusion.4
  215.9 1.6 convolution_add_fusion
  221.5 7.9 %scatter_custom_fusion = f32[256,16384]{1,0:T(8,128)} fusion(s32[16]{0:T(128)S(1)} %fusion.173, f32[16,16384]{1,0:T(8,128)S(1)} %reshape.172, f32[]{:T(128)} %constant.9.clone.1), kind=kCustom, calls=%fused_computation.2 | custom fusion | bytes 16777220 | tf_op jit(solution)/shard_map/scatter | solution.py:106
  231.4 6.6 %reduce-scatter.4.cloned.1.call-done = bf16[896,256]{1,0:T(8,128)(2,1)} async-done(((bf16[3584,256]{1,0:T(8,128)(2,1)}), bf16[896,256]{1,0:T(8,128)(2,1)}) %reduce-scatter.4.cloned.1.call-update) | async-done | bytes 458768
  238.0 2.0 copy.64
  240.0 229.0 %all-reduce.3.cloned.1.call-done = f32[256,16384]{1,0:T(8,128)} async-done(((f32[256,16384]{1,0:T(8,128)}), f32[256,16384]{1,0:T(8,128)}) %all-reduce.3.cloned.1.call-update) | async-done | bytes 16777232
  468.9 1.1 constant_dynamic-slice_fusion
  (165 shorter events, 23.5 us)
Async XLA Ops:
  7.2 37.8 %copy-start = (bf16[3584,128]{1,0:T(8,128)(2,1)S(1)}, bf16[3584,128]{1,0:T(8,128)(2,1)}, u32[]{:S(2)}) copy-start(bf16[3584,128]{1,0:T(8,128)(2,1)} %param.11) | copy-start | bytes 2752516
  7.2 46.6 %copy-start.17 = (bf16[256,896]{1,0:T(8,128)(2,1)S(1)}, bf16[256,896]{1,0:T(8,128)(2,1)}, u32[]{:S(2)}) copy-start(bf16[256,896]{1,0:T(8,128)(2,1)} %param.10) | copy-start | bytes 1376260
  7.2 47.0 %copy-start.16 = (bf16[3584,128]{1,0:T(8,128)(2,1)S(1)}, bf16[3584,128]{1,0:T(8,128)(2,1)}, u32[]{:S(2)}) copy-start(bf16[3584,128]{1,0:T(8,128)(2,1)} %param.12) | copy-start | bytes 2752516
  7.2 37.8 %all-gather.5.cloned.1.call-start = ((), (), s32[]{:S(2)}) async-start(), calls=%async_computation.1 | async-start | bytes 2293760 | tf_op jit(solution)/shard_map/all_gather | solution.py:32
  7.9 70.1 %all-gather.7.cloned.1.call-start = ((), (), s32[]{:S(2)}) async-start(), calls=%async_computation.2 | async-start | bytes 2293760 | tf_op jit(solution)/shard_map/all_gather | solution.py:33
  8.7 156.2 %all-gather.9.cloned.1.call-start = ((), (), s32[]{:S(2)}) async-start(), calls=%async_computation.3 | async-start | bytes 8519680 | tf_op jit(solution)/shard_map/all_gather | solution.py:46
  10.4 227.6 %reduce-scatter.4.cloned.1.call-start = ((), (), s32[]{:S(2)}) async-start(), calls=%async_computation.4 | async-start | bytes 2293760
  183.2 3.2 copy-start.19
  183.5 3.1 copy-start.21
  184.0 17.6 %copy-start.14 = (f32[1024,256]{1,0:T(8,128)}, f32[1024,256]{1,0:T(8,128)S(1)}, u32[]{:S(2)}) copy-start(f32[1024,256]{1,0:T(8,128)S(1)} %get-tuple-element.6) | copy-start | bytes 3145732
  184.4 17.6 %copy-start.12 = (f32[1024,256]{1,0:T(8,128)}, f32[1024,256]{1,0:T(8,128)S(1)}, u32[]{:S(2)}) copy-start(f32[1024,256]{1,0:T(8,128)S(1)} %get-tuple-element.10) | copy-start | bytes 3145732
  184.7 17.6 %copy-start.10 = (f32[1024,256]{1,0:T(8,128)}, f32[1024,256]{1,0:T(8,128)S(1)}, u32[]{:S(2)}) copy-start(f32[1024,256]{1,0:T(8,128)S(1)} %get-tuple-element.14) | copy-start | bytes 3145732
  185.1 17.6 %copy-start.8 = (f32[1024,256]{1,0:T(8,128)}, f32[1024,256]{1,0:T(8,128)S(1)}, u32[]{:S(2)}) copy-start(f32[1024,256]{1,0:T(8,128)S(1)} %get-tuple-element.18) | copy-start | bytes 3145732
  185.5 17.6 %copy-start.6 = (f32[1024,256]{1,0:T(8,128)}, f32[1024,256]{1,0:T(8,128)S(1)}, u32[]{:S(2)}) copy-start(f32[1024,256]{1,0:T(8,128)S(1)} %get-tuple-element.22) | copy-start | bytes 3145732
  185.8 17.7 %copy-start.4 = (f32[1024,256]{1,0:T(8,128)}, f32[1024,256]{1,0:T(8,128)S(1)}, u32[]{:S(2)}) copy-start(f32[1024,256]{1,0:T(8,128)S(1)} %get-tuple-element.26) | copy-start | bytes 3145732
  186.2 17.7 %copy-start.2 = (f32[1024,256]{1,0:T(8,128)}, f32[1024,256]{1,0:T(8,128)S(1)}, u32[]{:S(2)}) copy-start(f32[1024,256]{1,0:T(8,128)S(1)} %get-tuple-element.30) | copy-start | bytes 3145732
  186.4 3.3 copy-start.18
  203.1 2.2 slice-start
  203.5 2.6 slice-start.1
  206.1 4.7 copy-start.22
  210.7 3.9 copy-start.9
  210.8 4.3 copy-start.7
  210.8 258.2 %all-reduce.3.cloned.1.call-start = ((), (), s32[]{:S(2)}) async-start(), calls=%async_computation.5 | async-start | bytes 33554432
  213.0 2.5 copy-start.5
  215.1 2.5 copy-start.15
  215.1 2.5 copy-start.29
  215.5 2.5 copy-start.13
  215.5 2.5 copy-start.23
  215.9 2.5 copy-start.11
  215.9 2.5 copy-start.24
  218.4 1.6 copy-start.27
  229.4 241.5 %copy-start.1 = (bf16[3584,128]{1,0:T(8,128)(2,1)S(1)}, bf16[3584,128]{1,0:T(8,128)(2,1)}, u32[]{:S(2)}) copy-start(bf16[3584,128]{1,0:T(8,128)(2,1)} %param.11) | copy-start | bytes 2752516
  (5 other events, 6.2 us)
Sparse Core Ops, SparseCore 0:
  9.9 35.0 all-gather.4
  46.8 31.2 all-gather.6
  81.4 83.3 all-gather.8
  210.9 27.0 reduce-scatter.3
  241.5 227.3 all-reduce.2
where the time goes:
time: 478 us; the launch traced here: 477 us
  waiting for transfers between devices  373 us (78%)
  matrix products  47.3 us (10%)
  local copies, waits for them, and re-layouts  38.8 us (8%)
  between operations  15.2 us (3%)
    unnamed x7, waiting for transfers between devices  237 us
    all_gather x1, waiting for transfers between devices, local(): everything = lax.all_gather(local_cache, 'seq', axis=0, tiled=True)  80.6 us
    all_gather x1, waiting for transfers between devices, local(): hidden_piece = lax.all_gather(hidden_states, 'tp', axis=1, tiled=True)  33.5 us
    unnamed x70, local copies, waits for them, and re-layouts  22.3 us
    all_gather x1, waiting for transfers between devices, local(): grad_piece = lax.all_gather(out_grad, 'tp', axis=1, tiled=True)  21.7 us
  transfers between devices with their start and end apart: 5, of which 5 were waited for; matrix products, arithmetic and copies ran while one was open for 9% of the time, Pallas kernels for 0%

commit v1 on v0

--- a/solution.py
+++ b/solution.py
@@ -30,7 +30,12 @@
     flat_width = PBLK * 2 * cache_cols
     read_count = reads.shape[1]
     hidden_piece = lax.all_gather(hidden_states, "tp", axis=1, tiled=True)
-    grad_piece = lax.all_gather(out_grad, "tp", axis=1, tiled=True)
+    ring = [out_grad]
+    for hop in range(3):
+        ring.append(lax.ppermute(ring[-1], "tp", [(dev, (dev + 1) % 4) for dev in range(4)]))
+    grad_piece = jnp.roll(
+        jnp.concatenate(ring[::-1], axis=1), (lax.axis_index("tp") + 1) * ring[0].shape[1], axis=1
+    )
     new_keys = jnp.dot(hidden_piece, key_weight, preferred_element_type=jnp.float32)
     new_values = jnp.dot(hidden_piece, value_weight, preferred_element_type=jnp.float32)
     context_grad = lax.dot_general(

time: 478 us -> 457 us (0.956)
  waiting for transfers between devices: 373 us -> 353 us
  matrix products: 47.3 us -> 36.8 us
  starting transfers between devices: 0.2 us -> 6.22 us
    ppermute x0 -> x3, waiting for transfers between devices: none -> 40.9 us  [local(): lax.ppermute(ring[-1], 'tp', [(dev, (dev + 1) % 4) for dev in range(4)])]
    all_gather x1, waiting for transfers between devices: 33.5 us -> 0.01 us  [local(): hidden_piece = lax.all_gather(hidden_states, 'tp', axis=1, tiled=True)]
    all_gather x1 -> x0, waiting for transfers between devices: 21.7 us -> none  [local(): grad_piece = lax.all_gather(out_grad, 'tp', axis=1, tiled=True)]
    ppermute x0 -> x3, starting transfers between devices: none -> 6.06 us  [local(): lax.ppermute(ring[-1], 'tp', [(dev, (dev + 1) % 4) for dev in range(4)])]
    unnamed x70 -> x83, local copies, waits for them, and re-layouts: 22.3 us -> 25.1 us
    unnamed x7 -> x6, waiting for transfers between devices: 237 us -> 236 us
  transfers between devices with their start and end apart: 5 -> 7, of which waited for: 5 -> 6; matrix products, arithmetic and copies ran while one was open for 9% -> 7% of each run, Pallas kernels for 0% -> 0%
where the time goes in v1:
time: 457 us; the launch traced here: 456 us
  waiting for transfers between devices  353 us (77%)
  local copies, waits for them, and re-layouts  41.5 us (9%)
  matrix products  36.8 us (8%)
  between operations  15.2 us (3%)
  starting transfers between devices  6.22 us (1%)
    unnamed x6, waiting for transfers between devices  236 us
    all_gather x1, waiting for transfers between devices, local(): everything = lax.all_gather(local_cache, 'seq', axis=0, tiled=True)  76.5 us
    ppermute x3, waiting for transfers between devices, local(): lax.ppermute(ring[-1], 'tp', [(dev, (dev + 1) % 4) for dev in range(4)])  40.9 us
    unnamed x83, local copies, waits for them, and re-layouts  25.1 us
    dot_general x7, matrix products, local(): jnp.einsum('td,pd->tp', head_grads, values_prefix, preferred_element_type...  9.15 us
  transfers between devices with their start and end apart: 7, of which 6 were waited for; matrix products, arithmetic and copies ran while one was open for 7% of the time, Pallas kernels for 0%

profile of v1, /device:TPU:1, one launch (start us, length us, event | category | flops | bytes accessed | tf_op | source)
XLA Modules:
  0.0 455.9 jit_solution(3391914107465004568)
XLA Ops:
  8.0 0.9 pad_maximum_fusion.1
  9.7 2.2 collective-permute-start
  11.9 9.9 %collective-permute-done = bf16[256,896]{1,0:T(8,128)(2,1)S(1)} collective-permute-done((bf16[256,896]{1,0:T(8,128)(2,1)}, bf16[256,896]{1,0:T(8,128)(2,1)S(1)}, u32[]{:S(2)}, u32[]{:S(2)}) %collective-permute-start) | collective-permute-done | bytes 458784 | tf_op jit(solution)/shard_map/ppermute | solution.py:35
  21.7 1.6 collective-permute-start.1
  24.2 11.7 %collective-permute-done.1 = bf16[256,896]{1,0:T(8,128)(2,1)S(1)} collective-permute-done((bf16[256,896]{1,0:T(8,128)(2,1)S(1)}, bf16[256,896]{1,0:T(8,128)(2,1)S(1)}, u32[]{:S(2)}, u32[]{:S(2)}) %collective-permute-start.1) | collective-permute-done | bytes 458784 | tf_op jit(solution)/shard_map/ppermute | solution.py:35
  35.8 2.3 collective-permute-start.2
  38.4 19.4 %collective-permute-done.2 = bf16[256,896]{1,0:T(8,128)(2,1)S(1)} collective-permute-done((bf16[256,896]{1,0:T(8,128)(2,1)S(1)}, bf16[256,896]{1,0:T(8,128)(2,1)S(1)}, u32[]{:S(2)}, u32[]{:S(2)}) %collective-permute-start.2) | collective-permute-done | bytes 458784 | tf_op jit(solution)/shard_map/ppermute | solution.py:35
  58.4 2.9 fusion.4
  61.3 2.3 convolution_convert_fusion.2
  63.6 0.9 fusion.217
  64.5 0.9 fusion.219
  67.1 76.5 %all-gather.6.cloned.1.call-done = bf16[64,4,16384]{2,1,0:T(4,128)(2,1)} async-done(((bf16[1,4,16384]{2,1,0:T(4,128)(2,1)}), bf16[64,4,16384]{2,1,0:T(4,128)(2,1)}) %all-gather.6.cloned.1.call-update) | async-done | bytes 8388624 | tf_op jit(solution)/shard_map/all_gather | solution.py:51
  143.6 12.5 %reshape.177 = bf16[256,16384]{1,0:T(8,128)(2,1)} reshape(bf16[64,4,16384]{2,1,0:T(4,128)(2,1)} %all-gather.6.cloned.1.call-done) | data formatting | bytes 16777216
  156.1 5.8 %gather_fusion = bf16[16,16384]{1,0:T(8,128)(2,1)S(1)} fusion(bf16[256,16384]{1,0:T(8,128)(2,1)} %reshape.177, s32[1024]{0:T(1024)S(1)} %pad_clamp_fusion), kind=kCustom, calls=%fused_computation | custom fusion | bytes 1048640 | tf_op jit(solution)/shard_map/jit(_take)/gather | solution.py:52
  165.2 1.2 fusion.86
  166.4 1.3 fusion.55
  168.6 1.4 fusion.53
  170.8 1.3 fusion.51
  172.8 1.3 fusion.49
  174.8 1.3 fusion.47
  176.9 1.4 fusion.45
  179.0 1.3 fusion.43
  182.9 1.1 slice-done
  184.8 2.3 convolution_convert_fusion
  187.1 2.3 copy.63
  189.5 1.8 convolution_add_fusion.5
  194.2 1.4 convolution_add_fusion
  200.8 7.9 %scatter_custom_fusion = f32[256,16384]{1,0:T(8,128)} fusion(s32[16]{0:T(128)S(1)} %fusion.178, f32[16,16384]{1,0:T(8,128)S(1)} %reshape.172, f32[]{:T(128)} %constant.55.clone.1), kind=kCustom, calls=%fused_computation.2 | custom fusion | bytes 16777220 | tf_op jit(solution)/shard_map/scatter | solution.py:111
  210.6 6.1 %reduce-scatter.4.cloned.1.call-done = bf16[896,256]{1,0:T(8,128)(2,1)} async-done(((bf16[3584,256]{1,0:T(8,128)(2,1)}), bf16[896,256]{1,0:T(8,128)(2,1)}) %reduce-scatter.4.cloned.1.call-update) | async-done | bytes 458768
  216.7 2.0 copy.64
  218.7 228.7 %all-reduce.3.cloned.1.call-done = f32[256,16384]{1,0:T(8,128)} async-done(((f32[256,16384]{1,0:T(8,128)}), f32[256,16384]{1,0:T(8,128)}) %all-reduce.3.cloned.1.call-update) | async-done | bytes 16777232
  447.4 1.1 constant_dynamic-slice_fusion
  (182 shorter events, 26.2 us)
Async XLA Ops:
  7.2 54.1 %copy-start = (bf16[3584,128]{1,0:T(8,128)(2,1)S(1)}, bf16[3584,128]{1,0:T(8,128)(2,1)}, u32[]{:S(2)}) copy-start(bf16[3584,128]{1,0:T(8,128)(2,1)} %param.11) | copy-start | bytes 2752516
  7.2 50.8 %copy-start.18 = (bf16[256,896]{1,0:T(8,128)(2,1)S(1)}, bf16[256,896]{1,0:T(8,128)(2,1)}, u32[]{:S(2)}) copy-start(bf16[256,896]{1,0:T(8,128)(2,1)} %param.17) | copy-start | bytes 1376260
  7.2 54.1 %all-gather.4.cloned.1.call-start = ((), (), s32[]{:S(2)}) async-start(), calls=%async_computation.1 | async-start | bytes 2293760 | tf_op jit(solution)/shard_map/all_gather | solution.py:32
  7.9 135.6 %all-gather.6.cloned.1.call-start = ((), (), s32[]{:S(2)}) async-start(), calls=%async_computation.2 | async-start | bytes 8519680 | tf_op jit(solution)/shard_map/all_gather | solution.py:51
  9.6 207.0 %reduce-scatter.4.cloned.1.call-start = ((), (), s32[]{:S(2)}) async-start(), calls=%async_computation.3 | async-start | bytes 2293760
  9.7 12.1 %collective-permute-start = (bf16[256,896]{1,0:T(8,128)(2,1)}, bf16[256,896]{1,0:T(8,128)(2,1)S(1)}, u32[]{:S(2)}, u32[]{:S(2)}) collective-permute-start(bf16[256,896]{1,0:T(8,128)(2,1)} %param.17), channel_id=1, source_target_pairs={{0,1},{1,2},{2,3},{3,0},{4,5},{5,6},{6,7},{7,4},{8,9},{9,10},{10,1... | collective-permute-start | bytes 1376264 | tf_op jit(solution)/shard_map/ppermute | solution.py:35
  21.7 14.1 %collective-permute-start.1 = (bf16[256,896]{1,0:T(8,128)(2,1)S(1)}, bf16[256,896]{1,0:T(8,128)(2,1)S(1)}, u32[]{:S(2)}, u32[]{:S(2)}) collective-permute-start(bf16[256,896]{1,0:T(8,128)(2,1)S(1)} %collective-permute-done), channel_id=1, source_target_pairs={{0,1},{1,2},{2,3},{3,0},{4,5},{5,6},{6,7},{7,4},{8,9},{9,10},{10,1... | collective-permute-start | bytes 1376264 | tf_op jit(solution)/shard_map/ppermute | solution.py:35
  35.8 21.9 %collective-permute-start.2 = (bf16[256,896]{1,0:T(8,128)(2,1)S(1)}, bf16[256,896]{1,0:T(8,128)(2,1)S(1)}, u32[]{:S(2)}, u32[]{:S(2)}) collective-permute-start(bf16[256,896]{1,0:T(8,128)(2,1)S(1)} %collective-permute-done.1), channel_id=1, source_target_pairs={{0,1},{1,2},{2,3},{3,0},{4,5},{5,6},{6,7},{7,4},{8,9},{9,10},{10,1... | collective-permute-start | bytes 1376264 | tf_op jit(solution)/shard_map/ppermute | solution.py:35
  38.3 20.0 %copy-start.2 = (bf16[896,3584]{1,0:T(8,128)(2,1)S(1)}, bf16[896,3584]{1,0:T(8,128)(2,1)}, u32[]{:S(2)}) copy-start(bf16[896,3584]{1,0:T(8,128)(2,1)} %param.13) | copy-start | bytes 19267588
  58.4 5.2 %copy-start.20 = (bf16[256,896]{1,0:T(8,128)(2,1)S(1)}, bf16[256,896]{1,0:T(8,128)(2,1)}, u32[]{:S(2)}) copy-start(bf16[256,896]{1,0:T(8,128)(2,1)} %param.10) | copy-start | bytes 1376260
  61.3 5.2 %copy-start.19 = (bf16[3584,128]{1,0:T(8,128)(2,1)S(1)}, bf16[3584,128]{1,0:T(8,128)(2,1)}, u32[]{:S(2)}) copy-start(bf16[3584,128]{1,0:T(8,128)(2,1)} %param.12) | copy-start | bytes 2752516
  61.3 5.2 %copy-start.3 = (bf16[256,3584]{1,0:T(8,128)(2,1)S(1)}, bf16[256,3584]{1,0:T(8,128)(2,1)}, u32[]{:S(2)}) copy-start(bf16[256,3584]{1,0:T(8,128)(2,1)} %all-gather.4.cloned.1.call-done) | copy-start | bytes 5505028
  162.7 17.6 %copy-start.16 = (f32[1024,256]{1,0:T(8,128)}, f32[1024,256]{1,0:T(8,128)S(1)}, u32[]{:S(2)}) copy-start(f32[1024,256]{1,0:T(8,128)S(1)} %get-tuple-element.6) | copy-start | bytes 3145732
  163.0 17.6 %copy-start.14 = (f32[1024,256]{1,0:T(8,128)}, f32[1024,256]{1,0:T(8,128)S(1)}, u32[]{:S(2)}) copy-start(f32[1024,256]{1,0:T(8,128)S(1)} %get-tuple-element.10) | copy-start | bytes 3145732
  163.1 2.1 copy-start.22
  163.4 17.6 %copy-start.12 = (f32[1024,256]{1,0:T(8,128)}, f32[1024,256]{1,0:T(8,128)S(1)}, u32[]{:S(2)}) copy-start(f32[1024,256]{1,0:T(8,128)S(1)} %get-tuple-element.14) | copy-start | bytes 3145732
  163.4 1.8 copy-start.24
  163.8 17.6 %copy-start.10 = (f32[1024,256]{1,0:T(8,128)}, f32[1024,256]{1,0:T(8,128)S(1)}, u32[]{:S(2)}) copy-start(f32[1024,256]{1,0:T(8,128)S(1)} %get-tuple-element.18) | copy-start | bytes 3145732
  164.1 17.6 %copy-start.8 = (f32[1024,256]{1,0:T(8,128)}, f32[1024,256]{1,0:T(8,128)S(1)}, u32[]{:S(2)}) copy-start(f32[1024,256]{1,0:T(8,128)S(1)} %get-tuple-element.22) | copy-start | bytes 3145732
  164.5 17.6 %copy-start.6 = (f32[1024,256]{1,0:T(8,128)}, f32[1024,256]{1,0:T(8,128)S(1)}, u32[]{:S(2)}) copy-start(f32[1024,256]{1,0:T(8,128)S(1)} %get-tuple-element.26) | copy-start | bytes 3145732
  164.9 17.7 %copy-start.4 = (f32[1024,256]{1,0:T(8,128)}, f32[1024,256]{1,0:T(8,128)S(1)}, u32[]{:S(2)}) copy-start(f32[1024,256]{1,0:T(8,128)S(1)} %get-tuple-element.30) | copy-start | bytes 3145732
  166.4 2.0 copy-start.21
  181.8 2.2 slice-start
  182.2 2.6 slice-start.1
  187.1 2.4 copy-start.25
  189.4 2.2 copy-start.13
  189.5 257.9 %all-reduce.3.cloned.1.call-start = ((), (), s32[]{:S(2)}) async-start(), calls=%async_computation.4 | async-start | bytes 33554432
  193.8 1.8 copy-start.17
  193.8 1.8 copy-start.32
  194.2 1.8 copy-start.15
  194.2 1.9 copy-start.26
  208.7 240.7 %copy-start.1 = (bf16[3584,128]{1,0:T(8,128)(2,1)S(1)}, bf16[3584,128]{1,0:T(8,128)(2,1)}, u32[]{:S(2)}) copy-start(bf16[3584,128]{1,0:T(8,128)(2,1)} %param.11) | copy-start | bytes 2752516
  (10 other events, 12.7 us)
Sparse Core Ops, SparseCore 0:
  9.9 46.3 all-gather.3
  59.7 83.8 all-gather.5
  189.6 27.0 reduce-scatter.3
  220.2 227.1 all-reduce.2
